TPU v7x, 512 devices: a whole 4x4x16 slice. The times are simulated.
512 devices in a mesh: section: 8 (over z_lo), dp: 64 (over x, y, z_hi, core).
Axes of the slice: x: 4, y: 4, z: 16 (z_hi: 2, z_lo: 8; z = z_hi * 8 + z_lo), core: 2. Of those that a mesh axis runs over, the one named last changes fastest.
Arguments:
- section_input: bfloat16 [8, 256, 128, 512], P('section', 'dp'), may hold values from -6 to 6
- top_grad: bfloat16 [256, 128, 512], P('dp'), may hold values from -6 to 6
- conv_weight: bfloat16 [8, 3, 512, 512], P('section'), may hold values from -0.15625 to 0.15625
- step_table: bfloat16 [8, 50, 512], P('section'), may hold values from -4 to 4
- timesteps: int32 [256], P('dp'), may hold values from 0 to 49
- dilations: int32 [8], P('section'), may hold values from 1 to 32, as said below
Outputs:
- input_grad: bfloat16 [8, 256, 128, 512], P('section', 'dp')
- weight_grad: bfloat16 [8, 3, 512, 512], P('section')
- table_grad: bfloat16 [8, 50, 512], P('section')
Inputs may be any that keep to these rules, and one draw needn't show every extreme that they name: `dilations`: each is a power of two; some section has dilation 32 and some other section dilation 1.
All inputs are finite; a program needn't handle non-finite values.
Results may differ from a plain program's by a relative error of at most 0.014.
Values may be sent and summed in bfloat16 or wider, within the bound.
A program may use at most 64 MiB of HBM per device.

v0:
```python
import math

import jax
import jax.numpy as jnp
from jax import lax
from jax.sharding import PartitionSpec as P

DMAX = 32


def from_behind(value, axis, by):
    count = lax.axis_size(axis)
    pairs = [(i, i + by) for i in range(count) if 0 <= i + by < count]
    return lax.ppermute(value, axis, pairs)


def spread_taps(seq_rows, dilation, orientation):
    bins_count = seq_rows.shape[0]
    padded = jnp.pad(seq_rows, ((DMAX, DMAX), (0, 0)))
    pieces = []
    for tap_num in range(3):
        start = DMAX + orientation * (tap_num - 1) * dilation
        pieces.append(lax.dynamic_slice_in_dim(padded, start, bins_count, 0))
    return jnp.concatenate(pieces, axis=1)


def body(section_input, top_grad, conv_weight, step_table, timesteps, dilations):
    my_section = lax.axis_index("section")
    section_count = lax.axis_size("section")
    saved_input = section_input[0]
    conv_kernel = conv_weight[0]
    emb_table = step_table[0]
    dilation = dilations[0]
    micro_count, seq_bins, channels = saved_input.shape
    flat_weight = conv_kernel.reshape(3 * channels, channels)
    onehot = timesteps[:, None] == jnp.arange(emb_table.shape[0], dtype=jnp.int32)[None, :]
    onehot_float = onehot.astype(jnp.float32)
    step_embed = jnp.dot(onehot.astype(jnp.bfloat16), emb_table, preferred_element_type=jnp.float32)

    def advance(tick_num, state_in):
        received, grads_out, weight_acc, table_acc, stash_mixed, stash_delta = state_in
        micro_pos = tick_num - (section_count - 1 - my_section)
        active = (micro_pos >= 0) & (micro_pos < micro_count)
        micro_slot = jnp.clip(micro_pos, 0, micro_count - 1)
        top_rows = lax.dynamic_index_in_dim(top_grad, micro_slot, 0, keepdims=False)
        upstream = jnp.where(my_section == section_count - 1, top_rows, received)

        def run_layer(layer_state):
            grads_keep, weight_keep, table_keep, mixed_keep, delta_keep = layer_state
            input_rows = lax.dynamic_index_in_dim(saved_input, micro_slot, 0, keepdims=False)
            embed_row = lax.dynamic_index_in_dim(step_embed, micro_slot, 0, keepdims=True)
            mixed_rows = (input_rows.astype(jnp.float32) + embed_row).astype(jnp.bfloat16)
            fwd_taps = spread_taps(mixed_rows, dilation, 1)
            preact = jnp.dot(fwd_taps, flat_weight, preferred_element_type=jnp.float32)
            gate_value = jax.nn.sigmoid(preact)
            upstream_float = upstream.astype(jnp.float32)
            grad_pre = (upstream_float * gate_value * (1.0 + preact * (1.0 - gate_value))).astype(
                jnp.bfloat16
            )
            back_taps = spread_taps(grad_pre, dilation, -1).reshape(seq_bins, 3, channels)
            grad_mixed = jnp.einsum(
                "tko,kio->ti", back_taps, conv_kernel, preferred_element_type=jnp.float32
            )
            out_rows = (upstream_float + grad_mixed).astype(jnp.bfloat16)
            grads_keep = lax.dynamic_update_index_in_dim(grads_keep, out_rows, micro_slot, 0)
            step_row = lax.dynamic_index_in_dim(onehot_float, micro_slot, 0, keepdims=False)
            table_keep = table_keep + step_row[:, None] * jnp.sum(grad_mixed, axis=0)[None, :]
            weight_keep = weight_keep + lax.dot_general(
                fwd_taps, grad_pre, (((0,), (0,)), ((), ())), preferred_element_type=jnp.float32
            )
            return (out_rows, grads_keep, weight_keep, table_keep, mixed_keep, delta_keep)

        def skip_layer(layer_state):
            return (jnp.zeros_like(received),) + layer_state

        out_rows, grads_out, weight_acc, table_acc, stash_mixed, stash_delta = lax.cond(
            active,
            run_layer,
            skip_layer,
            (grads_out, weight_acc, table_acc, stash_mixed, stash_delta),
        )
        received = from_behind(out_rows, "section", -1)
        return (received, grads_out, weight_acc, table_acc, stash_mixed, stash_delta)

    stash_shape = (1, 8, channels)
    start_state = (
        jnp.zeros((seq_bins, channels), jnp.bfloat16),
        jnp.zeros((micro_count, seq_bins, channels), jnp.bfloat16),
        jnp.zeros((3 * channels, channels), jnp.float32),
        jnp.zeros(emb_table.shape, jnp.float32),
        jnp.zeros(stash_shape, jnp.bfloat16),
        jnp.zeros(stash_shape, jnp.bfloat16),
    )
    final_state = lax.fori_loop(0, section_count + micro_count - 1, advance, start_state)
    received, grads_out, weight_acc, table_acc, stash_mixed, stash_delta = final_state
    grad_scale = 1.0 / math.sqrt(micro_count * lax.axis_size("dp") * seq_bins)
    weight_block = weight_acc.reshape(3, channels, channels)
    weight_total, table_total = lax.psum((weight_block, table_acc), "dp")
    weight_out = (weight_total * grad_scale).astype(jnp.bfloat16)
    table_out = (table_total * grad_scale).astype(jnp.bfloat16)
    return (grads_out[None], weight_out[None], table_out[None])


def solution(mesh):
    placed = (
        P("section", "dp", None, None),
        P("dp", None, None),
        P("section", None, None, None),
        P("section", None, None),
        P("dp"),
        P("section"),
    )
    return jax.shard_map(
        body,
        mesh=mesh,
        in_specs=placed,
        out_specs=(
            P("section", "dp", None, None),
            P("section", None, None, None),
            P("section", None, None),
        ),
        check_vma=False,
    )
```

profile of v0, /device:TPU:1, one launch (start us, length us, event | category | flops | bytes accessed | tf_op | source)
XLA Modules:
  0.0 1371.2 jit_solution(11275048265676625598)
XLA Ops:
  11.4 251.2 %while.22 = (s32[]{:T(128)}, bf16[128,512]{1,0:T(8,128)(2,1)}, bf16[4,128,512]{2,1,0:T(8,128)(2,1)}, f32[1536,512]{1,0:T(8,128)S(1)}, f32[50,512]{1,0:T(8,128)},...) while((s32[]{:T(128)}, bf16[128,512]{1,0:T(8,128)(2,1)}, ...), condition=%wide.region_4.5_spmd.clone, body=%wide.region_0.4_spmd.clone.sunk | while | flops 609601408 | bytes 17125904 | solution.py:94
  13.4 5.6 collective-permute-done
  21.7 5.5 collective-permute-done
  30.0 5.2 collective-permute-done
  37.9 6.2 collective-permute-done
  46.8 6.5 collective-permute-done
  55.9 5.5 collective-permute-done
  64.1 105.5 %collective-permute-done = bf16[128,512]{1,0:T(8,128)(2,1)S(1)} collective-permute-done((bf16[128,512]{1,0:T(8,128)(2,1)}, bf16[128,512]{1,0:T(8,128)(2,1)S(1)}, u32[]{:S(2)}, u32[]{:S(2)}) %collective-permute-start) | collective-permute-done | bytes 131104 | tf_op jit(solution)/shard_map/while/body/eval_jaxpr/ppermute | solution.py:14
  170.3 15.5 %conditional.3 = (bf16[128,512]{1,0:T(8,128)(2,1)}, bf16[4,128,512]{2,1,0:T(8,128)(2,1)}, f32[1536,512]{1,0:T(8,128)S(1)}, f32[50,512]{1,0:T(8,128)}) conditional(s32[]{:T(128)} %convert_element_type.87, (bf16[4,128,512]{2,1,0:T(8,128)(2,1)}, f32[1536,512]{1,0:T(8,128)S(1)}, f32[50,512]{1,0:T(8,128)}) %tuple.67, (pred[]{:T(512)}, s32[]{:T(128)}, ...), branch_computations={%region_1.1_spmd, %region_2.3_spmd} | conditional | flops 609601024 | bytes 16076121 | solution.py:76
  176.8 1.9 copy.10
  178.7 3.0 bitcast_dynamic-update-slice_fusion
  187.1 5.8 collective-permute-done
  193.7 15.5 %conditional.3 = (bf16[128,512]{1,0:T(8,128)(2,1)}, bf16[4,128,512]{2,1,0:T(8,128)(2,1)}, f32[1536,512]{1,0:T(8,128)S(1)}, f32[50,512]{1,0:T(8,128)}) conditional(s32[]{:T(128)} %convert_element_type.87, (bf16[4,128,512]{2,1,0:T(8,128)(2,1)}, f32[1536,512]{1,0:T(8,128)S(1)}, f32[50,512]{1,0:T(8,128)}) %tuple.67, (pred[]{:T(512)}, s32[]{:T(128)}, ...), branch_computations={%region_1.1_spmd, %region_2.3_spmd} | conditional | flops 609601024 | bytes 16076121 | solution.py:76
  200.2 1.9 copy.10
  202.1 3.0 bitcast_dynamic-update-slice_fusion
  210.5 5.8 collective-permute-done
  217.1 15.5 %conditional.3 = (bf16[128,512]{1,0:T(8,128)(2,1)}, bf16[4,128,512]{2,1,0:T(8,128)(2,1)}, f32[1536,512]{1,0:T(8,128)S(1)}, f32[50,512]{1,0:T(8,128)}) conditional(s32[]{:T(128)} %convert_element_type.87, (bf16[4,128,512]{2,1,0:T(8,128)(2,1)}, f32[1536,512]{1,0:T(8,128)S(1)}, f32[50,512]{1,0:T(8,128)}) %tuple.67, (pred[]{:T(512)}, s32[]{:T(128)}, ...), branch_computations={%region_1.1_spmd, %region_2.3_spmd} | conditional | flops 609601024 | bytes 16076121 | solution.py:76
  225.5 3.0 bitcast_dynamic-update-slice_fusion
  233.9 5.8 collective-permute-done
  240.5 15.5 %conditional.3 = (bf16[128,512]{1,0:T(8,128)(2,1)}, bf16[4,128,512]{2,1,0:T(8,128)(2,1)}, f32[1536,512]{1,0:T(8,128)S(1)}, f32[50,512]{1,0:T(8,128)}) conditional(s32[]{:T(128)} %convert_element_type.87, (bf16[4,128,512]{2,1,0:T(8,128)(2,1)}, f32[1536,512]{1,0:T(8,128)S(1)}, f32[50,512]{1,0:T(8,128)}) %tuple.67, (pred[]{:T(512)}, s32[]{:T(128)}, ...), branch_computations={%region_1.1_spmd, %region_2.3_spmd} | conditional | flops 609601024 | bytes 16076121 | solution.py:76
  248.8 3.0 bitcast_dynamic-update-slice_fusion
  257.3 4.6 collective-permute-done
  264.3 1095.9 %all-reduce.5.cloned.1.call-done = (f32[3,512,512]{2,1,0:T(8,128)}, f32[50,512]{1,0:T(8,128)}) async-done(((f32[3,512,512]{2,1,0:T(8,128)}, f32[50,512]{1,0:T(8,128)}), (f32[3,512,512]{2,1,0:T(8,128)}, f32[50,512]{1,0:T(8,128)})) %all-reduce.5.cloned.1.call-update) | async-done | bytes 3248144 | tf_op jit(solution)/shard_map/psum | solution.py:98
  1360.2 3.5 fusion.11
  (132 shorter events, 76.1 us)
Async XLA Ops:
  7.2 0.8 copy-start
  7.2 4.2 copy-start.6
  7.2 1353.0 %all-reduce.5.cloned.1.call-start = ((), (), s32[]{:S(2)}) async-start(), calls=%async_computation | async-start | bytes 6520832 | tf_op jit(solution)/shard_map/psum | solution.py:98
  12.1 6.9 collective-permute-start
  19.1 0.7 copy-start.4
  20.4 6.8 collective-permute-start
  27.3 0.7 copy-start.4
  28.7 6.5 collective-permute-start
  35.2 0.7 copy-start.4
  36.6 7.5 collective-permute-start
  44.1 0.7 copy-start.4
  45.5 7.8 collective-permute-start
  54.6 6.8 collective-permute-start
  62.8 106.8 %collective-permute-start = (bf16[128,512]{1,0:T(8,128)(2,1)}, bf16[128,512]{1,0:T(8,128)(2,1)S(1)}, u32[]{:S(2)}, u32[]{:S(2)}) collective-permute-start(bf16[128,512]{1,0:T(8,128)(2,1)} %get-tuple-element.627), channel_id=1, source_target_pairs={{64,0},{128,64},{192,128},{256,192},{320,256},{384,320},{448,384},... | collective-permute-start | bytes 393224 | tf_op jit(solution)/shard_map/while/body/eval_jaxpr/ppermute | solution.py:14
  173.3 2.5 copy-start.3
  185.8 7.1 collective-permute-start
  196.7 2.5 copy-start.3
  209.2 7.1 collective-permute-start
  220.1 2.5 copy-start.3
  232.6 7.1 collective-permute-start
  243.5 2.5 copy-start.3
  256.0 5.9 collective-permute-start
  262.6 1.7 copy-start.1
  1360.2 3.5 copy-start.5
  (11 other events, 7.2 us)
Sparse Core Ops, SparseCore 0:
  264.4 1095.7 all-reduce.4
where the time goes:
time: 1370 us
  waiting for transfers between devices  1260 us (92%)
  local copies, waits for them, and re-layouts  27.8 us (2%)
  matrix products  26.5 us (2%)
  other arithmetic  22.2 us (2%)
  starting transfers between devices  14.2 us (1%)
  between operations  14.1 us (1%)
    psum x1, waiting for transfers between devices, body(): weight_total, table_total = lax.psum((weight_block, table_acc), 'dp')  1100 us
    ppermute x11, waiting for transfers between devices, from_behind(): return lax.ppermute(value, axis, pairs)  162 us
  transfers between devices with their start and end apart: 12, of which 12 were waited for; matrix products, arithmetic and copies ran while one was open for 0% of the time, Pallas kernels for 0%

commit v1 on v0

v1 whole, which is shorter than its diff:
```python
import functools
import math

import jax
import jax.numpy as jnp
from jax import lax
from jax.experimental import pallas as pl
from jax.experimental.pallas import tpu as pltpu
from jax.sharding import PartitionSpec as P

MESH = pl.DeviceIdType.MESH
NX, NY, NZ = 4, 4, 2
TABLE_ROWS = 64
PAD_ROWS = 128
F32 = jnp.float32
BF16 = jnp.bfloat16


def chain_kernel(
    x_ref, top_ref, w_ref, tab_ref, ts_ref, dil_ref, gout_ref, part_ref,
    wt, ht, fw, sp, bt, ups, downs, recv, tacc, top_sem, send_sem, recv_sem,
):
    sec = lax.axis_index("section")
    last = lax.axis_size("section") - 1
    groups, bins, chans = x_ref.shape
    steps = tab_ref.shape[0]
    dil = dil_ref[0]

    barrier = pltpu.get_barrier_semaphore()

    @pl.when(sec > 0)
    def _():
        pl.semaphore_signal(barrier, inc=1, device_id={"section": sec - 1}, device_id_type=MESH)

    @pl.when(sec < last)
    def _():
        pl.semaphore_signal(barrier, inc=1, device_id={"section": sec + 1}, device_id_type=MESH)

    top_copy = pltpu.make_async_copy(top_ref, recv, top_sem)

    @pl.when(sec == last)
    def _():
        top_copy.start()

    to_bin = lax.broadcasted_iota(jnp.int32, (bins, bins), 0)
    from_bin = lax.broadcasted_iota(jnp.int32, (bins, bins), 1)
    downs[...] = jnp.where(from_bin == to_bin - dil, 1.0, 0.0).astype(BF16)
    ups[...] = jnp.where(from_bin == to_bin + dil, 1.0, 0.0).astype(BF16)
    step_rows = lax.broadcasted_iota(jnp.int32, (steps, chans), 0)

    def mix(b, carry):
        row = pl.multiple_of(b * bins, bins)
        table = tab_ref[...].astype(F32)
        embed = jnp.sum(jnp.where(step_rows == ts_ref[b], table, 0.0), axis=0, keepdims=True)
        mixed = (x_ref[b].astype(F32) + embed).astype(BF16)
        fw[pl.ds(row, bins), chans : 2 * chans] = mixed
        fw[pl.ds(row, bins), 0:chans] = jnp.dot(
            downs[...], mixed, preferred_element_type=F32
        ).astype(BF16)
        fw[pl.ds(row, bins), 2 * chans :] = jnp.dot(
            ups[...], mixed, preferred_element_type=F32
        ).astype(BF16)
        return carry

    lax.fori_loop(0, groups, mix, 0)
    for c in range(0, chans, 256):
        preact = jnp.dot(fw[...], w_ref[:, c : c + 256], preferred_element_type=F32)
        gate = jax.nn.sigmoid(preact)
        sp[:, c : c + 256] = gate * (1.0 + preact * (1.0 - gate))
    for tap in range(3):
        wt[tap * chans : (tap + 1) * chans, :] = w_ref[tap * chans : (tap + 1) * chans, :].T
    tacc[...] = jnp.zeros_like(tacc)

    @pl.when(sec < last)
    def _():
        ht[...] = fw[:, chans : 2 * chans].T

    @pl.when(jnp.logical_and(sec > 0, sec < last))
    def _():
        pl.semaphore_wait(barrier, 2)

    @pl.when(jnp.logical_or(sec == 0, sec == last))
    def _():
        pl.semaphore_wait(barrier, 1)

    @pl.when(sec == last)
    def _():
        top_copy.wait()

    table_rows = lax.broadcasted_iota(jnp.int32, (TABLE_ROWS, chans), 0)

    def hop(b):
        return pltpu.make_async_remote_copy(
            src_ref=gout_ref.at[b],
            dst_ref=recv.at[b],
            send_sem=send_sem.at[b],
            recv_sem=recv_sem.at[b],
            device_id={"section": sec - 1},
            device_id_type=MESH,
        )

    def layer(b, carry):
        row = pl.multiple_of(b * bins, bins)

        @pl.when(sec < last)
        def _():
            hop(b).wait_recv()

        delta = (recv[b].astype(F32) * sp[pl.ds(row, bins), :]).astype(BF16)
        bt[pl.ds(row, bins), chans : 2 * chans] = delta
        bt[pl.ds(row, bins), 0:chans] = jnp.dot(
            ups[...], delta, preferred_element_type=F32
        ).astype(BF16)
        bt[pl.ds(row, bins), 2 * chans :] = jnp.dot(
            downs[...], delta, preferred_element_type=F32
        ).astype(BF16)
        grad = jnp.dot(bt[pl.ds(row, bins), :], wt[...], preferred_element_type=F32)
        gout_ref[b] = (recv[b].astype(F32) + grad).astype(BF16)

        @pl.when(sec > 0)
        def _():
            hop(b).start()

        total = jnp.sum(grad, axis=0, keepdims=True)
        tacc[...] += jnp.where(table_rows == ts_ref[b], total, 0.0)
        return carry

    lax.fori_loop(0, groups, layer, 0)

    @pl.when(sec == last)
    def _():
        ht[...] = fw[:, chans : 2 * chans].T

    rows = 3 * chans
    for tap in range(3):
        span = slice(tap * chans, (tap + 1) * chans)
        part_ref[span, :] = jnp.dot(ht[...], bt[:, span], preferred_element_type=F32).astype(BF16)
    part_ref[rows : rows + TABLE_ROWS, :] = tacc[...].astype(BF16)
    part_ref[rows + TABLE_ROWS :, :] = jnp.zeros((PAD_ROWS - TABLE_ROWS, chans), BF16)

    @pl.when(sec > 0)
    def _():
        for b in range(groups):
            hop(b).wait_send()


def chain(saved, top, weight, table, timesteps, dilations):
    groups, bins, chans = saved.shape
    vmem = pl.BlockSpec(memory_space=pltpu.VMEM)
    smem = pl.BlockSpec(memory_space=pltpu.SMEM)
    rows = 3 * chans
    return pl.pallas_call(
        chain_kernel,
        out_shape=(
            jax.ShapeDtypeStruct((groups, bins, chans), BF16),
            jax.ShapeDtypeStruct((rows + PAD_ROWS, chans), BF16),
        ),
        in_specs=[vmem, pl.BlockSpec(memory_space=pl.ANY), vmem, vmem, smem, smem],
        out_specs=(vmem, vmem),
        scratch_shapes=[
            pltpu.VMEM((rows, chans), BF16),
            pltpu.VMEM((chans, groups * bins), BF16),
            pltpu.VMEM((groups * bins, rows), BF16),
            pltpu.VMEM((groups * bins, chans), F32),
            pltpu.VMEM((groups * bins, rows), BF16),
            pltpu.VMEM((bins, bins), BF16),
            pltpu.VMEM((bins, bins), BF16),
            pltpu.VMEM((groups, bins, chans), BF16),
            pltpu.VMEM((TABLE_ROWS, chans), F32),
            pltpu.SemaphoreType.DMA,
            pltpu.SemaphoreType.DMA((groups,)),
            pltpu.SemaphoreType.DMA((groups,)),
        ],
        compiler_params=pltpu.CompilerParams(
            collective_id=0, has_side_effects=True, vmem_limit_bytes=40 << 20
        ),
        name="chain",
    )(saved, top, weight, table, timesteps, dilations)


def reduce_kernel(
    scale, part_ref, out_ref,
    half_in, half, quarter_in, quarter, piece_in, piece, far_in,
    send_sem, recv_sem,
):
    dp = lax.axis_index("dp")
    core = dp % 2
    zpos = (dp // 2) % NZ
    ypos = (dp // (2 * NZ)) % NY
    xpos = dp // (2 * NZ * NY)
    side = NX
    half_rows, chans = half.shape
    quarter_rows = quarter.shape[0]
    width = piece.shape[1]

    def index_of(x, y, z, c):
        return ((x * NY + y) * NZ + z) * 2 + c

    first = xpos * (1 - core) + ypos * core
    second = ypos * (1 - core) + xpos * core

    def at(a, b):
        return index_of(a * (1 - core) + b * core, b * (1 - core) + a * core, zpos, core)

    mate = index_of(xpos, ypos, zpos, 1 - core)
    far = index_of(xpos, ypos, (zpos + 1) % NZ, core)
    peers_a = [(first + j) % side for j in range(1, side)]
    peers_b = [(second + j) % side for j in range(1, side)]
    everyone = [mate, far] + [at(a, second) for a in peers_a] + [at(first, b) for b in peers_b]

    barrier = pltpu.get_barrier_semaphore()
    for who in everyone:
        pl.semaphore_signal(barrier, inc=1, device_id={"dp": who}, device_id_type=MESH)
    pl.semaphore_wait(barrier, len(everyone))

    def send(src, dst, slot, who):
        copy = pltpu.make_async_remote_copy(
            src_ref=src, dst_ref=dst, send_sem=send_sem.at[slot], recv_sem=recv_sem.at[slot],
            device_id={"dp": who}, device_id_type=MESH,
        )
        copy.start()
        return copy

    def rows_at(start, size):
        return pl.ds(pl.multiple_of(start, 16), size)

    def cols_at(start, size):
        return pl.ds(pl.multiple_of(start, 128), size)

    def by_rows(count, step, body):
        def run(i, carry):
            body(pl.multiple_of(i * step, step))
            return carry
        lax.fori_loop(0, count // step, run, 0)

    pending = []
    copy = send(part_ref.at[rows_at((1 - core) * half_rows, half_rows), :], half_in, 0, mate)
    copy.wait_recv()
    pending.append(copy)

    def add_half(r):
        own = part_ref[pl.ds(pl.multiple_of(core * half_rows + r, 16), 16), :].astype(F32)
        half[pl.ds(r, 16), :] = (own + half_in[pl.ds(r, 16), :].astype(F32)).astype(BF16)
    by_rows(half_rows, 16, add_half)

    copies = [
        send(half.at[rows_at(a * quarter_rows, quarter_rows), :], quarter_in.at[j], 1 + j, at(a, second))
        for j, a in enumerate(peers_a)
    ]
    for copy in copies:
        copy.wait_recv()
    pending += copies

    def add_quarter(r):
        total = half[pl.ds(pl.multiple_of(first * quarter_rows + r, 16), 16), :].astype(F32)
        for j in range(side - 1):
            total += quarter_in[j, pl.ds(r, 16), :].astype(F32)
        quarter[pl.ds(r, 16), :] = total.astype(BF16)
    by_rows(quarter_rows, 16, add_quarter)

    copies = [
        send(quarter.at[:, cols_at(b * width, width)], piece_in.at[j], 4 + j, at(first, b))
        for j, b in enumerate(peers_b)
    ]
    for copy in copies:
        copy.wait_recv()
    pending += copies

    total = quarter[:, cols_at(second * width, width)].astype(F32)
    for j in range(side - 1):
        total += piece_in[j].astype(F32)
    piece[...] = total.astype(BF16)

    copy = send(piece, far_in, 7, far)
    copy.wait_recv()
    pending.append(copy)
    row_base = core * half_rows + first * quarter_rows
    mine = (rows_at(row_base, quarter_rows), cols_at(second * width, width))
    out_ref[mine] = ((piece[...].astype(F32) + far_in[...].astype(F32)) * scale).astype(BF16)

    copies = [
        send(out_ref.at[mine], out_ref.at[mine], 8 + j, at(first, b)) for j, b in enumerate(peers_b)
    ]
    for copy in copies:
        copy.wait_recv()
    pending += copies

    band = (rows_at(row_base, quarter_rows), slice(None))
    copies = [
        send(out_ref.at[band], out_ref.at[band], 11 + j, at(a, second)) for j, a in enumerate(peers_a)
    ]
    for copy in copies:
        copy.wait_recv()
    pending += copies

    block = (rows_at(core * half_rows, half_rows), slice(None))
    copy = send(out_ref.at[block], out_ref.at[block], 14, mate)
    copy.wait_recv()
    pending.append(copy)
    for copy in pending:
        copy.wait_send()


def reduce_all(part, scale):
    rows, chans = part.shape
    half, quarter, width = rows // 2, rows // 2 // NX, chans // NY
    vmem = pl.BlockSpec(memory_space=pltpu.VMEM)
    return pl.pallas_call(
        functools.partial(reduce_kernel, scale),
        out_shape=jax.ShapeDtypeStruct((rows, chans), BF16),
        in_specs=[vmem],
        out_specs=vmem,
        scratch_shapes=[
            pltpu.VMEM((half, chans), BF16),
            pltpu.VMEM((half, chans), BF16),
            pltpu.VMEM((NX - 1, quarter, chans), BF16),
            pltpu.VMEM((quarter, chans), BF16),
            pltpu.VMEM((NX - 1, quarter, width), BF16),
            pltpu.VMEM((quarter, width), BF16),
            pltpu.VMEM((quarter, width), BF16),
            pltpu.SemaphoreType.DMA((15,)),
            pltpu.SemaphoreType.DMA((15,)),
        ],
        compiler_params=pltpu.CompilerParams(
            collective_id=1, has_side_effects=True, vmem_limit_bytes=32 << 20
        ),
        name="reduce_all",
    )(part)


def body(section_input, top_grad, conv_weight, step_table, timesteps, dilations):
    taps, chans = conv_weight.shape[1], conv_weight.shape[2]
    groups, bins = top_grad.shape[0], top_grad.shape[1]
    weight = conv_weight.reshape(taps * chans, chans)
    grads, part = chain(section_input[0], top_grad, weight, step_table[0], timesteps, dilations)
    scale = 1.0 / math.sqrt(groups * lax.axis_size("dp") * bins)
    total = reduce_all(part, scale)
    weight_out = total[: taps * chans].reshape(1, taps, chans, chans)
    table_out = total[taps * chans : taps * chans + step_table.shape[1]][None]
    return grads[None], weight_out, table_out


def solution(mesh):
    placed = (
        P("section", "dp", None, None),
        P("dp", None, None),
        P("section", None, None, None),
        P("section", None, None),
        P("dp"),
        P("section"),
    )
    return jax.shard_map(
        body,
        mesh=mesh,
        in_specs=placed,
        out_specs=(
            P("section", "dp", None, None),
            P("section", None, None, None),
            P("section", None, None),
        ),
        check_vma=False,
    )
```

time: 1370 us -> 113 us (0.08)
  waiting for transfers between devices: 1260 us -> 0 us
  Pallas kernels: 0 us -> 104 us
  matrix products: 26.5 us -> 0 us
  other arithmetic: 22.2 us -> 0 us
  local copies, waits for them, and re-layouts: 27.8 us -> 7.62 us
  starting transfers between devices: 14.2 us -> 0 us
    psum x1 -> x0, waiting for transfers between devices: 1100 us -> none  [body(): weight_total, table_total = lax.psum((weight_block, table_acc), 'dp')]
    ppermute x11 -> x0, waiting for transfers between devices: 162 us -> none  [from_behind(): return lax.ppermute(value, axis, pairs)]
    pallas_call x0 -> x2, Pallas kernels: none -> 104 us  [the longest x1 57.5 us: chain(): pl.pallas_call(chain_kernel, out_shape=(jax.ShapeDtypeStruct((groups, bin...]
    dot_general x13 -> x0, matrix products: 26.5 us -> none  [the longest x4 11.9 us: run_layer(): jnp.einsum('tko,kio->ti', back_taps, conv_kernel, preferred_element_type=...]
    ppermute x11 -> x0, starting transfers between devices: 14.1 us -> none  [from_behind(): return lax.ppermute(value, axis, pairs)]
  transfers between devices with their start and end apart: 12 -> 0, of which waited for: 12 -> 0; matrix products, arithmetic and copies ran while one was open for 0% -> 0% of each run, Pallas kernels for 0% -> 0%
where the time goes in v1:
time: 113 us; the launch traced here: 112 us
  Pallas kernels  104 us (92%)
  local copies, waits for them, and re-layouts  7.62 us (7%)
  between operations  1.31 us (1%)
    pallas_call x1, Pallas kernels, chain(): pl.pallas_call(chain_kernel, out_shape=(jax.ShapeDtypeStruct((groups, bin...  57.5 us
    pallas_call x1, Pallas kernels, reduce_all(): pl.pallas_call(functools.partial(reduce_kernel, scale), out_shape=jax.Sha...  46 us
    unnamed x11, local copies, waits for them, and re-layouts  5.75 us

profile of v1, /device:TPU:1, one launch (start us, length us, event | category | flops | bytes accessed | tf_op | source)
XLA Modules:
  0.0 112.5 jit_solution(9514039256616489929)
XLA Ops:
  1.3 0.0 copy-start
  1.3 1.4 %copy-done = bf16[1,3,512,512]{3,2,1,0:T(8,128)(2,1)S(1)} copy-done((bf16[1,3,512,512]{3,2,1,0:T(8,128)(2,1)S(1)}, bf16[1,3,512,512]{3,2,1,0:T(8,128)(2,1)}, u32[]{:S(2)}) %copy-start) | copy-done | bytes 1572888
  2.7 0.0 copy-start.1
  2.7 1.0 copy-done.1
  3.7 0.0 copy-start.2
  3.7 1.0 copy-done.2
  4.8 0.0 copy-start.3
  4.8 0.8 copy-done.3
  5.6 0.0 copy-start.4
  5.6 0.7 copy-done.4
  6.2 57.5 %chain.1 = (bf16[4,128,512]{2,1,0:T(8,128)(2,1)S(1)}, bf16[1664,512]{1,0:T(8,128)(2,1)S(1)}) custom-call(bf16[4,128,512]{2,1,0:T(8,128)(2,1)S(1)} %bitcast.8, bf16[4,128,512]{2,1,0:T(8,128)(2,1)S(1)} %copy-done.2, bf16[1536,512]{1,0:T(8,128)(2,1)S(1)} %bitcast.7, bf16[50,512]{1,0:T(8,128)(2,1)S(1)} %bitcast.10, s32[4]{0:T(128)S(1)} %copy-done.4, ...), custom_call_target="tpu_custom_call" | custom-call | tf_op jit(solution)/shard_map/chain/pallas_call | solution.py:152
  63.8 46.0 %reduce_all.1 = bf16[1664,512]{1,0:T(8,128)(2,1)S(1)} custom-call(bf16[1664,512]{1,0:T(8,128)(2,1)S(1)} %get-tuple-element.6.part_ref), custom_call_target="tpu_custom_call" | custom-call | tf_op jit(solution)/shard_map/reduce_all/pallas_call | solution.py:308
  109.8 0.6 slice_bitcast_fusion
  110.5 1.2 %slice.6 = bf16[1536,512]{1,0:T(8,128)(2,1)} slice(bf16[1664,512]{1,0:T(8,128)(2,1)S(1)} %reduce_all.1), slice={[0:1536], [0:512]} | slice | bytes 3145728 | tf_op jit(solution)/shard_map/slice | solution.py:338
  111.7 0.8 copy.11
Async XLA Ops:
  1.3 1.4 %copy-start = (bf16[1,3,512,512]{3,2,1,0:T(8,128)(2,1)S(1)}, bf16[1,3,512,512]{3,2,1,0:T(8,128)(2,1)}, u32[]{:S(2)}) copy-start(bf16[1,3,512,512]{3,2,1,0:T(8,128)(2,1)} %param.8) | copy-start | bytes 4718596
  2.7 1.0 copy-start.1
  3.7 1.0 copy-start.2
  4.8 0.8 copy-start.3
  5.6 0.7 copy-start.4

commit v2 on v1

--- a/solution.py
+++ b/solution.py
@@ -12,6 +12,8 @@
 NX, NY, NZ = 4, 4, 2
 TABLE_ROWS = 64
 PAD_ROWS = 128
+CHUNKS = ((0, 64), (64, 112), (112, 160), (160, 208))
+STAGES = 10
 F32 = jnp.float32
 BF16 = jnp.bfloat16
 
@@ -180,7 +182,7 @@
 
 def reduce_kernel(
     scale, part_ref, out_ref,
-    half_in, half, quarter_in, quarter, piece_in, piece, far_in,
+    half_in, half, relay_in, relay, near_in, next_in, quarter, piece_in, piece, far_in,
     send_sem, recv_sem,
 ):
     dp = lax.axis_index("dp")
@@ -189,8 +191,6 @@
     ypos = (dp // (2 * NZ)) % NY
     xpos = dp // (2 * NZ * NY)
     side = NX
-    half_rows, chans = half.shape
-    quarter_rows = quarter.shape[0]
     width = piece.shape[1]
 
     def index_of(x, y, z, c):
@@ -204,122 +204,145 @@
 
     mate = index_of(xpos, ypos, zpos, 1 - core)
     far = index_of(xpos, ypos, (zpos + 1) % NZ, core)
-    peers_a = [(first + j) % side for j in range(1, side)]
-    peers_b = [(second + j) % side for j in range(1, side)]
-    everyone = [mate, far] + [at(a, second) for a in peers_a] + [at(first, b) for b in peers_b]
+    ahead, behind = (first + 1) % side, (first + side - 1) % side
+    opposite = (first + 2) % side
+    peers = [(second + j) % side for j in range(1, side)]
+    everyone = [mate, far, at(ahead, second), at(behind, second)] + [at(first, b) for b in peers]
 
     barrier = pltpu.get_barrier_semaphore()
     for who in everyone:
         pl.semaphore_signal(barrier, inc=1, device_id={"dp": who}, device_id_type=MESH)
     pl.semaphore_wait(barrier, len(everyone))
 
-    def send(src, dst, slot, who):
+    pending = []
+
+    def send(src, dst, chunk, slot, who):
         copy = pltpu.make_async_remote_copy(
-            src_ref=src, dst_ref=dst, send_sem=send_sem.at[slot], recv_sem=recv_sem.at[slot],
+            src_ref=src, dst_ref=dst,
+            send_sem=send_sem.at[chunk, slot], recv_sem=recv_sem.at[chunk, slot],
             device_id={"dp": who}, device_id_type=MESH,
         )
         copy.start()
+        pending.append(copy)
         return copy
-
-    def rows_at(start, size):
-        return pl.ds(pl.multiple_of(start, 16), size)
 
     def cols_at(start, size):
         return pl.ds(pl.multiple_of(start, 128), size)
 
-    def by_rows(count, step, body):
-        def run(i, carry):
-            body(pl.multiple_of(i * step, step))
-            return carry
-        lax.fori_loop(0, count // step, run, 0)
-
-    pending = []
-    copy = send(part_ref.at[rows_at((1 - core) * half_rows, half_rows), :], half_in, 0, mate)
-    copy.wait_recv()
-    pending.append(copy)
-
-    def add_half(r):
-        own = part_ref[pl.ds(pl.multiple_of(core * half_rows + r, 16), 16), :].astype(F32)
-        half[pl.ds(r, 16), :] = (own + half_in[pl.ds(r, 16), :].astype(F32)).astype(BF16)
-    by_rows(half_rows, 16, add_half)
-
-    copies = [
-        send(half.at[rows_at(a * quarter_rows, quarter_rows), :], quarter_in.at[j], 1 + j, at(a, second))
-        for j, a in enumerate(peers_a)
-    ]
-    for copy in copies:
+    mine, theirs = core * side, (1 - core) * side
+    own_cols = cols_at(second * width, width)
+
+    def steps(chunk):
+        start, stop = CHUNKS[chunk]
+        rows = pl.ds(start, stop - start)
+        onward, backward = (ahead, behind) if chunk % 2 == 0 else (behind, ahead)
+
+        def forward_to_mate(slot, quarter_id):
+            ref = out_ref.at[mine + quarter_id, rows, :]
+            return send(ref, ref, chunk, slot, mate)
+
+        copy = send(
+            part_ref.at[pl.ds(theirs, side), rows, :], half_in.at[:, rows, :], chunk, 0, mate
+        )
+        yield
         copy.wait_recv()
-    pending += copies
-
-    def add_quarter(r):
-        total = half[pl.ds(pl.multiple_of(first * quarter_rows + r, 16), 16), :].astype(F32)
+        for q in range(side):
+            own = part_ref[mine + q, rows, :].astype(F32)
+            half[q, rows, :] = (own + half_in[q, rows, :].astype(F32)).astype(BF16)
+        passed = send(
+            half.at[opposite, rows, :], relay_in.at[rows, :], chunk, 1, at(onward, second)
+        )
+        direct = send(
+            half.at[backward, rows, :], near_in.at[rows, :], chunk, 2, at(backward, second)
+        )
+        yield
+        passed.wait_recv()
+        relay[rows, :] = (
+            half[onward, rows, :].astype(F32) + relay_in[rows, :].astype(F32)
+        ).astype(BF16)
+        joined = send(relay.at[rows, :], next_in.at[rows, :], chunk, 3, at(onward, second))
+        yield
+        direct.wait_recv()
+        joined.wait_recv()
+        quarter[rows, :] = (
+            half[first, rows, :].astype(F32)
+            + near_in[rows, :].astype(F32)
+            + next_in[rows, :].astype(F32)
+        ).astype(BF16)
+        copies = [
+            send(
+                quarter.at[rows, cols_at(b * width, width)], piece_in.at[j, rows, :],
+                chunk, 4 + j, at(first, b),
+            )
+            for j, b in enumerate(peers)
+        ]
+        yield
+        for copy in copies:
+            copy.wait_recv()
+        total = quarter[rows, own_cols].astype(F32)
         for j in range(side - 1):
-            total += quarter_in[j, pl.ds(r, 16), :].astype(F32)
-        quarter[pl.ds(r, 16), :] = total.astype(BF16)
-    by_rows(quarter_rows, 16, add_quarter)
-
-    copies = [
-        send(quarter.at[:, cols_at(b * width, width)], piece_in.at[j], 4 + j, at(first, b))
-        for j, b in enumerate(peers_b)
-    ]
-    for copy in copies:
+            total += piece_in[j, rows, :].astype(F32)
+        piece[rows, :] = total.astype(BF16)
+        copy = send(piece.at[rows, :], far_in.at[rows, :], chunk, 7, far)
+        yield
         copy.wait_recv()
-    pending += copies
-
-    total = quarter[:, cols_at(second * width, width)].astype(F32)
-    for j in range(side - 1):
-        total += piece_in[j].astype(F32)
-    piece[...] = total.astype(BF16)
-
-    copy = send(piece, far_in, 7, far)
-    copy.wait_recv()
-    pending.append(copy)
-    row_base = core * half_rows + first * quarter_rows
-    mine = (rows_at(row_base, quarter_rows), cols_at(second * width, width))
-    out_ref[mine] = ((piece[...].astype(F32) + far_in[...].astype(F32)) * scale).astype(BF16)
-
-    copies = [
-        send(out_ref.at[mine], out_ref.at[mine], 8 + j, at(first, b)) for j, b in enumerate(peers_b)
-    ]
-    for copy in copies:
-        copy.wait_recv()
-    pending += copies
-
-    band = (rows_at(row_base, quarter_rows), slice(None))
-    copies = [
-        send(out_ref.at[band], out_ref.at[band], 11 + j, at(a, second)) for j, a in enumerate(peers_a)
-    ]
-    for copy in copies:
-        copy.wait_recv()
-    pending += copies
-
-    block = (rows_at(core * half_rows, half_rows), slice(None))
-    copy = send(out_ref.at[block], out_ref.at[block], 14, mate)
-    copy.wait_recv()
-    pending.append(copy)
+        out_ref[mine + first, rows, own_cols] = (
+            (piece[rows, :].astype(F32) + far_in[rows, :].astype(F32)) * scale
+        ).astype(BF16)
+        block = out_ref.at[mine + first, rows, own_cols]
+        copies = [send(block, block, chunk, 8 + j, at(first, b)) for j, b in enumerate(peers)]
+        yield
+        for copy in copies:
+            copy.wait_recv()
+        band = out_ref.at[mine + first, rows, :]
+        one = send(band, band, chunk, 11, at(onward, second))
+        two = send(band, band, chunk, 12, at(backward, second))
+        final = [forward_to_mate(14, first)]
+        yield
+        one.wait_recv()
+        band = out_ref.at[mine + backward, rows, :]
+        three = send(band, band, chunk, 13, at(onward, second))
+        final.append(forward_to_mate(15, backward))
+        two.wait_recv()
+        final.append(forward_to_mate(16, onward))
+        yield
+        three.wait_recv()
+        final.append(forward_to_mate(17, opposite))
+        yield
+        for copy in final:
+            copy.wait_recv()
+
+    running = [steps(chunk) for chunk in range(len(CHUNKS))]
+    for tick in range(STAGES + len(CHUNKS) - 1):
+        for chunk, run in enumerate(running):
+            if 0 <= tick - chunk < STAGES:
+                next(run, None)
     for copy in pending:
         copy.wait_send()
 
 
 def reduce_all(part, scale):
-    rows, chans = part.shape
-    half, quarter, width = rows // 2, rows // 2 // NX, chans // NY
+    quarters, rows, chans = part.shape
+    width = chans // NY
     vmem = pl.BlockSpec(memory_space=pltpu.VMEM)
     return pl.pallas_call(
         functools.partial(reduce_kernel, scale),
-        out_shape=jax.ShapeDtypeStruct((rows, chans), BF16),
+        out_shape=jax.ShapeDtypeStruct(part.shape, BF16),
         in_specs=[vmem],
         out_specs=vmem,
         scratch_shapes=[
-            pltpu.VMEM((half, chans), BF16),
-            pltpu.VMEM((half, chans), BF16),
-            pltpu.VMEM((NX - 1, quarter, chans), BF16),
-            pltpu.VMEM((quarter, chans), BF16),
-            pltpu.VMEM((NX - 1, quarter, width), BF16),
-            pltpu.VMEM((quarter, width), BF16),
-            pltpu.VMEM((quarter, width), BF16),
-            pltpu.SemaphoreType.DMA((15,)),
-            pltpu.SemaphoreType.DMA((15,)),
+            pltpu.VMEM((NX, rows, chans), BF16),
+            pltpu.VMEM((NX, rows, chans), BF16),
+            pltpu.VMEM((rows, chans), BF16),
+            pltpu.VMEM((rows, chans), BF16),
+            pltpu.VMEM((rows, chans), BF16),
+            pltpu.VMEM((rows, chans), BF16),
+            pltpu.VMEM((rows, chans), BF16),
+            pltpu.VMEM((NY - 1, rows, width), BF16),
+            pltpu.VMEM((rows, width), BF16),
+            pltpu.VMEM((rows, width), BF16),
+            pltpu.SemaphoreType.DMA((len(CHUNKS), 18)),
+            pltpu.SemaphoreType.DMA((len(CHUNKS), 18)),
         ],
         compiler_params=pltpu.CompilerParams(
             collective_id=1, has_side_effects=True, vmem_limit_bytes=32 << 20
@@ -334,7 +357,7 @@
     weight = conv_weight.reshape(taps * chans, chans)
     grads, part = chain(section_input[0], top_grad, weight, step_table[0], timesteps, dilations)
     scale = 1.0 / math.sqrt(groups * lax.axis_size("dp") * bins)
-    total = reduce_all(part, scale)
+    total = reduce_all(part.reshape(2 * NX, -1, chans), scale).reshape(-1, chans)
     weight_out = total[: taps * chans].reshape(1, taps, chans, chans)
     table_out = total[taps * chans : taps * chans + step_table.shape[1]][None]
     return grads[None], weight_out, table_out

time: 113 us -> 128 us (1.13)
  Pallas kernels: 104 us -> 118 us
    pallas_call x1, Pallas kernels: 46 us -> 61.5 us  [reduce_all(): pl.pallas_call(functools.partial(reduce_kernel, scale), out_shape=jax.Sha...]
where the time goes in v2:
time: 128 us; the launch traced here: 127 us
  Pallas kernels  118 us (92%)
  local copies, waits for them, and re-layouts  7.62 us (6%)
  between operations  1.31 us (1%)
    pallas_call x1, Pallas kernels, reduce_all(): pl.pallas_call(functools.partial(reduce_kernel, scale), out_shape=jax.Sha...  61.5 us
    pallas_call x1, Pallas kernels, chain(): pl.pallas_call(chain_kernel, out_shape=(jax.ShapeDtypeStruct((groups, bin...  57 us
    unnamed x11, local copies, waits for them, and re-layouts  5.75 us

profile of v2, /device:TPU:1, one launch (start us, length us, event | category | flops | bytes accessed | tf_op | source)
XLA Modules:
  0.0 127.4 jit_solution(14759977736516513323)
XLA Ops:
  1.3 0.0 copy-start
  1.3 1.4 %copy-done = bf16[1,3,512,512]{3,2,1,0:T(8,128)(2,1)S(1)} copy-done((bf16[1,3,512,512]{3,2,1,0:T(8,128)(2,1)S(1)}, bf16[1,3,512,512]{3,2,1,0:T(8,128)(2,1)}, u32[]{:S(2)}) %copy-start) | copy-done | bytes 1572888
  2.7 0.0 copy-start.1
  2.7 1.0 copy-done.1
  3.7 0.0 copy-start.2
  3.7 1.0 copy-done.2
  4.8 0.0 copy-start.3
  4.8 0.8 copy-done.3
  5.6 0.0 copy-start.4
  5.6 0.7 copy-done.4
  6.2 57.0 %chain.1 = (bf16[4,128,512]{2,1,0:T(8,128)(2,1)S(1)}, bf16[1664,512]{1,0:T(8,128)(2,1)S(1)}) custom-call(bf16[4,128,512]{2,1,0:T(8,128)(2,1)S(1)} %bitcast.13, bf16[4,128,512]{2,1,0:T(8,128)(2,1)S(1)} %copy-done.2, bf16[1536,512]{1,0:T(8,128)(2,1)S(1)} %bitcast.12, bf16[50,512]{1,0:T(8,128)(2,1)S(1)} %bitcast.15, s32[4]{0:T(128)S(1)} %copy-done.4, ...), custom_call_target="tpu_custom_call" | custom-call | tf_op jit(solution)/shard_map/chain/pallas_call | solution.py:154
  63.3 61.5 %reduce_all.1 = bf16[8,208,512]{2,1,0:T(8,128)(2,1)S(1)} custom-call(bf16[8,208,512]{2,1,0:T(8,128)(2,1)S(1)} %bitcast.11), custom_call_target="tpu_custom_call" | custom-call | tf_op jit(solution)/shard_map/reduce_all/pallas_call | solution.py:328
  124.8 0.6 slice_bitcast_fusion
  125.4 1.2 slice.8
  126.6 0.8 copy.11
Async XLA Ops:
  1.3 1.4 %copy-start = (bf16[1,3,512,512]{3,2,1,0:T(8,128)(2,1)S(1)}, bf16[1,3,512,512]{3,2,1,0:T(8,128)(2,1)}, u32[]{:S(2)}) copy-start(bf16[1,3,512,512]{3,2,1,0:T(8,128)(2,1)} %param.8) | copy-start | bytes 4718596
  2.7 1.0 copy-start.1
  3.7 1.0 copy-start.2
  4.8 0.8 copy-start.3
  5.6 0.7 copy-start.4

commit v3 on v2

--- a/solution.py
+++ b/solution.py
@@ -19,8 +19,9 @@
 
 
 def chain_kernel(
-    x_ref, top_ref, w_ref, tab_ref, ts_ref, dil_ref, gout_ref, part_ref,
-    wt, ht, fw, sp, bt, ups, downs, recv, tacc, top_sem, send_sem, recv_sem,
+    x_hbm, top_hbm, w_hbm, tab_hbm, ts_ref, dil_ref, gout_ref, part_ref,
+    x_ref, w_ref, tab_ref, wt, ht, fw, sp, bt, ups, downs, recv, tacc,
+    load_sem, send_sem, recv_sem,
 ):
     sec = lax.axis_index("section")
     last = lax.axis_size("section") - 1
@@ -38,7 +39,13 @@
     def _():
         pl.semaphore_signal(barrier, inc=1, device_id={"section": sec + 1}, device_id_type=MESH)
 
-    top_copy = pltpu.make_async_copy(top_ref, recv, top_sem)
+    table_copy = pltpu.make_async_copy(tab_hbm, tab_ref, load_sem.at[0])
+    x_copy = pltpu.make_async_copy(x_hbm, x_ref, load_sem.at[1])
+    weight_copy = pltpu.make_async_copy(w_hbm, w_ref, load_sem.at[2])
+    top_copy = pltpu.make_async_copy(top_hbm, recv, load_sem.at[3])
+    table_copy.start()
+    x_copy.start()
+    weight_copy.start()
 
     @pl.when(sec == last)
     def _():
@@ -64,7 +71,10 @@
         ).astype(BF16)
         return carry
 
+    table_copy.wait()
+    x_copy.wait()
     lax.fori_loop(0, groups, mix, 0)
+    weight_copy.wait()
     for c in range(0, chans, 256):
         preact = jnp.dot(fw[...], w_ref[:, c : c + 256], preferred_element_type=F32)
         gate = jax.nn.sigmoid(preact)
@@ -89,42 +99,49 @@
     def _():
         top_copy.wait()
 
-    table_rows = lax.broadcasted_iota(jnp.int32, (TABLE_ROWS, chans), 0)
-
-    def hop(b):
+    table_rows = lax.broadcasted_iota(jnp.int32, (TABLE_ROWS, chans // 2), 0)
+
+    half = chans // 2
+
+    def hop(b, h):
+        span = pl.ds(h * half, half)
         return pltpu.make_async_remote_copy(
-            src_ref=gout_ref.at[b],
-            dst_ref=recv.at[b],
-            send_sem=send_sem.at[b],
-            recv_sem=recv_sem.at[b],
+            src_ref=gout_ref.at[b, :, span],
+            dst_ref=recv.at[b, :, span],
+            send_sem=send_sem.at[b, h],
+            recv_sem=recv_sem.at[b, h],
             device_id={"section": sec - 1},
             device_id_type=MESH,
         )
 
     def layer(b, carry):
-        row = pl.multiple_of(b * bins, bins)
-
-        @pl.when(sec < last)
-        def _():
-            hop(b).wait_recv()
-
-        delta = (recv[b].astype(F32) * sp[pl.ds(row, bins), :]).astype(BF16)
-        bt[pl.ds(row, bins), chans : 2 * chans] = delta
-        bt[pl.ds(row, bins), 0:chans] = jnp.dot(
-            ups[...], delta, preferred_element_type=F32
-        ).astype(BF16)
-        bt[pl.ds(row, bins), 2 * chans :] = jnp.dot(
-            downs[...], delta, preferred_element_type=F32
-        ).astype(BF16)
-        grad = jnp.dot(bt[pl.ds(row, bins), :], wt[...], preferred_element_type=F32)
-        gout_ref[b] = (recv[b].astype(F32) + grad).astype(BF16)
-
-        @pl.when(sec > 0)
-        def _():
-            hop(b).start()
-
-        total = jnp.sum(grad, axis=0, keepdims=True)
-        tacc[...] += jnp.where(table_rows == ts_ref[b], total, 0.0)
+        rows = pl.ds(pl.multiple_of(b * bins, bins), bins)
+        for h in range(2):
+            lo, hi = h * half, (h + 1) * half
+
+            @pl.when(sec < last)
+            def _():
+                hop(b, h).wait_recv()
+
+            delta = (recv[b, :, lo:hi].astype(F32) * sp[rows, lo:hi]).astype(BF16)
+            bt[rows, chans + lo : chans + hi] = delta
+            bt[rows, lo:hi] = jnp.dot(
+                ups[...], delta, preferred_element_type=F32
+            ).astype(BF16)
+            bt[rows, 2 * chans + lo : 2 * chans + hi] = jnp.dot(
+                downs[...], delta, preferred_element_type=F32
+            ).astype(BF16)
+        for h in range(2):
+            lo, hi = h * half, (h + 1) * half
+            grad = jnp.dot(bt[rows, :], wt[:, lo:hi], preferred_element_type=F32)
+            gout_ref[b, :, lo:hi] = (recv[b, :, lo:hi].astype(F32) + grad).astype(BF16)
+
+            @pl.when(sec > 0)
+            def _():
+                hop(b, h).start()
+
+            total = jnp.sum(grad, axis=0, keepdims=True)
+            tacc[:, lo:hi] += jnp.where(table_rows == ts_ref[b], total, 0.0)
         return carry
 
     lax.fori_loop(0, groups, layer, 0)
@@ -143,12 +160,14 @@
     @pl.when(sec > 0)
     def _():
         for b in range(groups):
-            hop(b).wait_send()
+            for h in range(2):
+                hop(b, h).wait_send()
 
 
 def chain(saved, top, weight, table, timesteps, dilations):
     groups, bins, chans = saved.shape
     vmem = pl.BlockSpec(memory_space=pltpu.VMEM)
+    hbm = pl.BlockSpec(memory_space=pltpu.HBM)
     smem = pl.BlockSpec(memory_space=pltpu.SMEM)
     rows = 3 * chans
     return pl.pallas_call(
@@ -157,9 +176,12 @@
             jax.ShapeDtypeStruct((groups, bins, chans), BF16),
             jax.ShapeDtypeStruct((rows + PAD_ROWS, chans), BF16),
         ),
-        in_specs=[vmem, pl.BlockSpec(memory_space=pl.ANY), vmem, vmem, smem, smem],
+        in_specs=[hbm, hbm, hbm, hbm, smem, smem],
         out_specs=(vmem, vmem),
         scratch_shapes=[
+            pltpu.VMEM(saved.shape, BF16),
+            pltpu.VMEM(weight.shape, BF16),
+            pltpu.VMEM(table.shape, BF16),
             pltpu.VMEM((rows, chans), BF16),
             pltpu.VMEM((chans, groups * bins), BF16),
             pltpu.VMEM((groups * bins, rows), BF16),
@@ -169,12 +191,12 @@
             pltpu.VMEM((bins, bins), BF16),
             pltpu.VMEM((groups, bins, chans), BF16),
             pltpu.VMEM((TABLE_ROWS, chans), F32),
-            pltpu.SemaphoreType.DMA,
-            pltpu.SemaphoreType.DMA((groups,)),
-            pltpu.SemaphoreType.DMA((groups,)),
+            pltpu.SemaphoreType.DMA((4,)),
+            pltpu.SemaphoreType.DMA((groups, 2)),
+            pltpu.SemaphoreType.DMA((groups, 2)),
         ],
         compiler_params=pltpu.CompilerParams(
-            collective_id=0, has_side_effects=True, vmem_limit_bytes=40 << 20
+            collective_id=0, has_side_effects=True, vmem_limit_bytes=67043328
         ),
         name="chain",
     )(saved, top, weight, table, timesteps, dilations)
@@ -313,10 +335,9 @@
             copy.wait_recv()
 
     running = [steps(chunk) for chunk in range(len(CHUNKS))]
-    for tick in range(STAGES + len(CHUNKS) - 1):
-        for chunk, run in enumerate(running):
-            if 0 <= tick - chunk < STAGES:
-                next(run, None)
+    for stage in range(STAGES):
+        for run in running:
+            next(run, None)
     for copy in pending:
         copy.wait_send()
 

time: 128 us -> 109 us (0.85)
  Pallas kernels: 118 us -> 103 us
  local copies, waits for them, and re-layouts: 7.62 us -> 4.12 us
    pallas_call x1, Pallas kernels: 61.5 us -> 43.7 us  [reduce_all(): pl.pallas_call(functools.partial(reduce_kernel, scale), out_shape=jax.Sha...]
    unnamed x11 -> x5, local copies, waits for them, and re-layouts: 5.75 us -> 2.24 us
    pallas_call x1, Pallas kernels: 57 us -> 59.7 us  [chain(): pl.pallas_call(chain_kernel, out_shape=(jax.ShapeDtypeStruct((groups, bin...]
where the time goes in v3:
time: 109 us
  Pallas kernels  103 us (94%)
  local copies, waits for them, and re-layouts  4.12 us (4%)
  between operations  1.31 us (1%)
    pallas_call x1, Pallas kernels, chain(): pl.pallas_call(chain_kernel, out_shape=(jax.ShapeDtypeStruct((groups, bin...  59.7 us
    pallas_call x1, Pallas kernels, reduce_all(): pl.pallas_call(functools.partial(reduce_kernel, scale), out_shape=jax.Sha...  43.7 us
    unnamed x5, local copies, waits for them, and re-layouts  2.24 us

profile of v3, /device:TPU:1, one launch (start us, length us, event | category | flops | bytes accessed | tf_op | source)
XLA Modules:
  0.0 108.8 jit_solution(2558803178121675896)
XLA Ops:
  1.3 59.7 %chain.1 = (bf16[4,128,512]{2,1,0:T(8,128)(2,1)}, bf16[1664,512]{1,0:T(8,128)(2,1)}) custom-call(bf16[4,128,512]{2,1,0:T(8,128)(2,1)} %bitcast.14, bf16[4,128,512]{2,1,0:T(8,128)(2,1)} %top_hbm.1, bf16[1536,512]{1,0:T(8,128)(2,1)} %bitcast.12, bf16[50,512]{1,0:T(8,128)(2,1)} %bitcast.16, s32[4]{0:T(128)} %ts_ref.1, s32[1]{0:T(128)S(6)} %copy.10.dil_ref), custom_call_target="tpu_custom_call" | custom-call | tf_op jit(solution)/shard_map/chain/pallas_call | solution.py:173
  61.0 0.0 copy-start
  61.0 1.4 %copy-done = bf16[1664,512]{1,0:T(8,128)(2,1)S(1)} copy-done((bf16[1664,512]{1,0:T(8,128)(2,1)S(1)}, bf16[1664,512]{1,0:T(8,128)(2,1)}, u32[]{:S(2)}) %copy-start) | copy-done | bytes 1703960
  62.4 43.7 %reduce_all.1 = bf16[8,208,512]{2,1,0:T(8,128)(2,1)S(1)} custom-call(bf16[8,208,512]{2,1,0:T(8,128)(2,1)S(1)} %bitcast.11), custom_call_target="tpu_custom_call" | custom-call | tf_op jit(solution)/shard_map/reduce_all/pallas_call | solution.py:349
  106.1 0.0 copy-start.1
  106.1 0.6 slice_bitcast_fusion
  106.7 1.2 %slice.8 = bf16[1536,512]{1,0:T(8,128)(2,1)} slice(bf16[1664,512]{1,0:T(8,128)(2,1)S(1)} %bitcast.10), slice={[0:1536], [0:512]} | slice | bytes 3145728 | tf_op jit(solution)/shard_map/slice | solution.py:382
  108.0 0.0 copy-done.1
  108.0 0.8 copy.11
Async XLA Ops:
  61.0 1.5 %copy-start = (bf16[1664,512]{1,0:T(8,128)(2,1)S(1)}, bf16[1664,512]{1,0:T(8,128)(2,1)}, u32[]{:S(2)}) copy-start(bf16[1664,512]{1,0:T(8,128)(2,1)} %get-tuple-element.6) | copy-start | bytes 5111812
  106.1 1.9 %copy-start.1 = (bf16[4,128,512]{2,1,0:T(8,128)(2,1)S(1)}, bf16[4,128,512]{2,1,0:T(8,128)(2,1)}, u32[]{:S(2)}) copy-start(bf16[4,128,512]{2,1,0:T(8,128)(2,1)} %get-tuple-element.5) | copy-start | bytes 1572868

commit v4 on v3

--- a/solution.py
+++ b/solution.py
@@ -18,13 +18,14 @@
 BF16 = jnp.bfloat16
 
 
-def chain_kernel(
-    x_hbm, top_hbm, w_hbm, tab_hbm, ts_ref, dil_ref, gout_ref, part_ref,
+def chain_part(
+    greeted, x_hbm, top_hbm, w_hbm, tab_hbm, ts_ref, dil_ref, gout_ref, part_ref,
     x_ref, w_ref, tab_ref, wt, ht, fw, sp, bt, ups, downs, recv, tacc,
     load_sem, send_sem, recv_sem,
 ):
     sec = lax.axis_index("section")
     last = lax.axis_size("section") - 1
+    core = lax.axis_index("dp") % 2
     groups, bins, chans = x_ref.shape
     steps = tab_ref.shape[0]
     dil = dil_ref[0]
@@ -83,17 +84,17 @@
         wt[tap * chans : (tap + 1) * chans, :] = w_ref[tap * chans : (tap + 1) * chans, :].T
     tacc[...] = jnp.zeros_like(tacc)
 
-    @pl.when(sec < last)
+    @pl.when(jnp.logical_or(sec < last, core == 1))
     def _():
         ht[...] = fw[:, chans : 2 * chans].T
 
     @pl.when(jnp.logical_and(sec > 0, sec < last))
     def _():
-        pl.semaphore_wait(barrier, 2)
+        pl.semaphore_wait(barrier, greeted + 2)
 
     @pl.when(jnp.logical_or(sec == 0, sec == last))
     def _():
-        pl.semaphore_wait(barrier, 1)
+        pl.semaphore_wait(barrier, greeted + 1)
 
     @pl.when(sec == last)
     def _():
@@ -146,16 +147,25 @@
 
     lax.fori_loop(0, groups, layer, 0)
 
-    @pl.when(sec == last)
+    @pl.when(jnp.logical_and(sec == last, core == 0))
     def _():
         ht[...] = fw[:, chans : 2 * chans].T
 
-    rows = 3 * chans
+    quarter_rows = part_ref.shape[1]
+
+    def put(base, value):
+        done = 0
+        while done < value.shape[0]:
+            q, r = divmod(base + done, quarter_rows)
+            size = min(value.shape[0] - done, quarter_rows - r)
+            part_ref[q, r : r + size, :] = value[done : done + size, :]
+            done += size
+
     for tap in range(3):
         span = slice(tap * chans, (tap + 1) * chans)
-        part_ref[span, :] = jnp.dot(ht[...], bt[:, span], preferred_element_type=F32).astype(BF16)
-    part_ref[rows : rows + TABLE_ROWS, :] = tacc[...].astype(BF16)
-    part_ref[rows + TABLE_ROWS :, :] = jnp.zeros((PAD_ROWS - TABLE_ROWS, chans), BF16)
+        put(tap * chans, jnp.dot(ht[...], bt[:, span], preferred_element_type=F32).astype(BF16))
+    put(3 * chans, tacc[...].astype(BF16))
+    put(3 * chans + TABLE_ROWS, jnp.zeros((PAD_ROWS - TABLE_ROWS, chans), BF16))
 
     @pl.when(sec > 0)
     def _():
@@ -164,46 +174,8 @@
                 hop(b, h).wait_send()
 
 
-def chain(saved, top, weight, table, timesteps, dilations):
-    groups, bins, chans = saved.shape
-    vmem = pl.BlockSpec(memory_space=pltpu.VMEM)
-    hbm = pl.BlockSpec(memory_space=pltpu.HBM)
-    smem = pl.BlockSpec(memory_space=pltpu.SMEM)
-    rows = 3 * chans
-    return pl.pallas_call(
-        chain_kernel,
-        out_shape=(
-            jax.ShapeDtypeStruct((groups, bins, chans), BF16),
-            jax.ShapeDtypeStruct((rows + PAD_ROWS, chans), BF16),
-        ),
-        in_specs=[hbm, hbm, hbm, hbm, smem, smem],
-        out_specs=(vmem, vmem),
-        scratch_shapes=[
-            pltpu.VMEM(saved.shape, BF16),
-            pltpu.VMEM(weight.shape, BF16),
-            pltpu.VMEM(table.shape, BF16),
-            pltpu.VMEM((rows, chans), BF16),
-            pltpu.VMEM((chans, groups * bins), BF16),
-            pltpu.VMEM((groups * bins, rows), BF16),
-            pltpu.VMEM((groups * bins, chans), F32),
-            pltpu.VMEM((groups * bins, rows), BF16),
-            pltpu.VMEM((bins, bins), BF16),
-            pltpu.VMEM((bins, bins), BF16),
-            pltpu.VMEM((groups, bins, chans), BF16),
-            pltpu.VMEM((TABLE_ROWS, chans), F32),
-            pltpu.SemaphoreType.DMA((4,)),
-            pltpu.SemaphoreType.DMA((groups, 2)),
-            pltpu.SemaphoreType.DMA((groups, 2)),
-        ],
-        compiler_params=pltpu.CompilerParams(
-            collective_id=0, has_side_effects=True, vmem_limit_bytes=67043328
-        ),
-        name="chain",
-    )(saved, top, weight, table, timesteps, dilations)
-
-
-def reduce_kernel(
-    scale, part_ref, out_ref,
+def reduce_part(
+    scale, run_chain, part_ref, out_ref,
     half_in, half, relay_in, relay, near_in, next_in, quarter, piece_in, piece, far_in,
     send_sem, recv_sem,
 ):
@@ -234,7 +206,7 @@
     barrier = pltpu.get_barrier_semaphore()
     for who in everyone:
         pl.semaphore_signal(barrier, inc=1, device_id={"dp": who}, device_id_type=MESH)
-    pl.semaphore_wait(barrier, len(everyone))
+    run_chain(len(everyone))
 
     pending = []
 
@@ -342,16 +314,55 @@
         copy.wait_send()
 
 
-def reduce_all(part, scale):
-    quarters, rows, chans = part.shape
+def kernel(scale, *refs):
+    operands, (gout_hbm, out_ref), scratch = refs[:6], refs[6:8], refs[8:]
+    gout_ref, part_ref, out_sem = scratch[:3]
+    chain_scratch, reduce_scratch = scratch[3:18], scratch[18:]
+    gout_copy = pltpu.make_async_copy(gout_ref, gout_hbm, out_sem)
+
+    def run_chain(greeted):
+        chain_part(greeted, *operands, gout_ref, part_ref, *chain_scratch)
+        gout_copy.start()
+
+    reduce_part(scale, run_chain, part_ref, out_ref, *reduce_scratch)
+    gout_copy.wait()
+
+
+def backward(saved, top, weight, table, timesteps, dilations, scale):
+    groups, bins, chans = saved.shape
+    vmem = pl.BlockSpec(memory_space=pltpu.VMEM)
+    hbm = pl.BlockSpec(memory_space=pltpu.HBM)
+    smem = pl.BlockSpec(memory_space=pltpu.SMEM)
+    taps = 3 * chans
+    rows = (taps + PAD_ROWS) // (2 * NX)
     width = chans // NY
-    vmem = pl.BlockSpec(memory_space=pltpu.VMEM)
     return pl.pallas_call(
-        functools.partial(reduce_kernel, scale),
-        out_shape=jax.ShapeDtypeStruct(part.shape, BF16),
-        in_specs=[vmem],
-        out_specs=vmem,
+        functools.partial(kernel, scale),
+        out_shape=(
+            jax.ShapeDtypeStruct((groups, bins, chans), BF16),
+            jax.ShapeDtypeStruct((2 * NX, rows, chans), BF16),
+        ),
+        in_specs=[hbm, hbm, hbm, hbm, smem, smem],
+        out_specs=(hbm, vmem),
         scratch_shapes=[
+            pltpu.VMEM((groups, bins, chans), BF16),
+            pltpu.VMEM((2 * NX, rows, chans), BF16),
+            pltpu.SemaphoreType.DMA,
+            pltpu.VMEM(saved.shape, BF16),
+            pltpu.VMEM(weight.shape, BF16),
+            pltpu.VMEM(table.shape, BF16),
+            pltpu.VMEM((taps, chans), BF16),
+            pltpu.VMEM((chans, groups * bins), BF16),
+            pltpu.VMEM((groups * bins, taps), BF16),
+            pltpu.VMEM((groups * bins, chans), F32),
+            pltpu.VMEM((groups * bins, taps), BF16),
+            pltpu.VMEM((bins, bins), BF16),
+            pltpu.VMEM((bins, bins), BF16),
+            pltpu.VMEM((groups, bins, chans), BF16),
+            pltpu.VMEM((TABLE_ROWS, chans), F32),
+            pltpu.SemaphoreType.DMA((4,)),
+            pltpu.SemaphoreType.DMA((groups, 2)),
+            pltpu.SemaphoreType.DMA((groups, 2)),
             pltpu.VMEM((NX, rows, chans), BF16),
             pltpu.VMEM((NX, rows, chans), BF16),
             pltpu.VMEM((rows, chans), BF16),
@@ -366,19 +377,21 @@
             pltpu.SemaphoreType.DMA((len(CHUNKS), 18)),
         ],
         compiler_params=pltpu.CompilerParams(
-            collective_id=1, has_side_effects=True, vmem_limit_bytes=32 << 20
+            collective_id=0, has_side_effects=True, vmem_limit_bytes=67043328
         ),
-        name="reduce_all",
-    )(part)
+        name="backward",
+    )(saved, top, weight, table, timesteps, dilations)
 
 
 def body(section_input, top_grad, conv_weight, step_table, timesteps, dilations):
     taps, chans = conv_weight.shape[1], conv_weight.shape[2]
     groups, bins = top_grad.shape[0], top_grad.shape[1]
     weight = conv_weight.reshape(taps * chans, chans)
-    grads, part = chain(section_input[0], top_grad, weight, step_table[0], timesteps, dilations)
     scale = 1.0 / math.sqrt(groups * lax.axis_size("dp") * bins)
-    total = reduce_all(part.reshape(2 * NX, -1, chans), scale).reshape(-1, chans)
+    grads, total = backward(
+        section_input[0], top_grad, weight, step_table[0], timesteps, dilations, scale
+    )
+    total = total.reshape(-1, chans)
     weight_out = total[: taps * chans].reshape(1, taps, chans, chans)
     table_out = total[taps * chans : taps * chans + step_table.shape[1]][None]
     return grads[None], weight_out, table_out

time: 109 us -> 105 us (0.963)
  Pallas kernels: 103 us -> 98.5 us
    pallas_call x2 -> x1, Pallas kernels: 103 us -> 98.5 us  [backward(): pl.pallas_call(functools.partial(kernel, scale), out_shape=(jax.ShapeDtyp...]
    unnamed x5 -> x3, local copies, waits for them, and re-layouts: 2.24 us -> 0.8 us
    slice x1, local copies, waits for them, and re-layouts: 1.24 us -> 2.65 us  [body(): weight_out = total[:taps * chans].reshape(1, taps, chans, chans)]
where the time goes in v4:
time: 105 us
  Pallas kernels  98.5 us (94%)
  local copies, waits for them, and re-layouts  4.95 us (5%)
  between operations  1.3 us (1%)
    pallas_call x1, Pallas kernels, backward(): pl.pallas_call(functools.partial(kernel, scale), out_shape=(jax.ShapeDtyp...  98.5 us
    slice x1, local copies, waits for them, and re-layouts, body(): weight_out = total[:taps * chans].reshape(1, taps, chans, chans)  2.65 us

profile of v4, /device:TPU:1, one launch (start us, length us, event | category | flops | bytes accessed | tf_op | source)
XLA Modules:
  0.0 104.7 jit_solution(17062310073989530075)
XLA Ops:
  1.3 98.5 %backward.1 = (bf16[4,128,512]{2,1,0:T(8,128)(2,1)}, bf16[8,208,512]{2,1,0:T(8,128)(2,1)}) custom-call(bf16[4,128,512]{2,1,0:T(8,128)(2,1)} %bitcast.12, bf16[4,128,512]{2,1,0:T(8,128)(2,1)} %refs_1_.1, bf16[1536,512]{1,0:T(8,128)(2,1)} %bitcast.8, bf16[50,512]{1,0:T(8,128)(2,1)} %bitcast.14, s32[4]{0:T(128)} %refs_4_.1, s32[1]{0:T(128)S(6)} %copy.10.refs_5_), custom_call_target="tpu_custom_call" | custom-call | tf_op jit(solution)/shard_map/backward/pallas_call | solution.py:339
  99.7 0.0 copy-start
  99.8 1.5 %slice_bitcast_fusion = bf16[1,50,512]{2,1,0:T(8,128)(2,1)} fusion(bf16[1664,512]{1,0:T(8,128)(2,1)} %bitcast.10), kind=kLoop, calls=%fused_computation | loop fusion | bytes 102400 | tf_op jit(solution)/shard_map/broadcast_in_dim | solution.py:396
  101.3 2.7 %slice.8 = bf16[1536,512]{1,0:T(8,128)(2,1)} slice(bf16[1664,512]{1,0:T(8,128)(2,1)} %bitcast.11), slice={[0:1536], [0:512]} | slice | bytes 3145728 | tf_op jit(solution)/shard_map/slice | solution.py:395
  103.9 0.0 copy-done
  103.9 0.8 copy.11
Async XLA Ops:
  99.7 4.2 %copy-start = (bf16[4,128,512]{2,1,0:T(8,128)(2,1)S(1)}, bf16[4,128,512]{2,1,0:T(8,128)(2,1)}, u32[]{:S(2)}) copy-start(bf16[4,128,512]{2,1,0:T(8,128)(2,1)} %get-tuple-element.5) | copy-start | bytes 1572868

commit v5 on v4

--- a/solution.py
+++ b/solution.py
@@ -12,7 +12,7 @@
 NX, NY, NZ = 4, 4, 2
 TABLE_ROWS = 64
 PAD_ROWS = 128
-CHUNKS = ((0, 64), (64, 112), (112, 160), (160, 208))
+CHUNKS = ((0, 112), (112, 208))
 STAGES = 10
 F32 = jnp.float32
 BF16 = jnp.bfloat16

time: 105 us -> 105 us (level)
  no operation moved by 1% of the time
where the time goes in v5:
time: 105 us
  Pallas kernels  98.3 us (94%)
  local copies, waits for them, and re-layouts  4.95 us (5%)
  between operations  1.3 us (1%)
    pallas_call x1, Pallas kernels, backward(): pl.pallas_call(functools.partial(kernel, scale), out_shape=(jax.ShapeDtyp...  98.3 us
    slice x1, local copies, waits for them, and re-layouts, body(): weight_out = total[:taps * chans].reshape(1, taps, chans, chans)  2.65 us

profile of v5, /device:TPU:1, one launch (start us, length us, event | category | flops | bytes accessed | tf_op | source)
XLA Modules:
  0.0 104.6 jit_solution(12194523704851773725)
XLA Ops:
  1.3 98.3 %backward.1 = (bf16[4,128,512]{2,1,0:T(8,128)(2,1)}, bf16[8,208,512]{2,1,0:T(8,128)(2,1)}) custom-call(bf16[4,128,512]{2,1,0:T(8,128)(2,1)} %bitcast.12, bf16[4,128,512]{2,1,0:T(8,128)(2,1)} %refs_1_.1, bf16[1536,512]{1,0:T(8,128)(2,1)} %bitcast.8, bf16[50,512]{1,0:T(8,128)(2,1)} %bitcast.14, s32[4]{0:T(128)} %refs_4_.1, s32[1]{0:T(128)S(6)} %copy.10.refs_5_), custom_call_target="tpu_custom_call" | custom-call | tf_op jit(solution)/shard_map/backward/pallas_call | solution.py:339
  99.6 0.0 copy-start
  99.6 1.5 %slice_bitcast_fusion = bf16[1,50,512]{2,1,0:T(8,128)(2,1)} fusion(bf16[1664,512]{1,0:T(8,128)(2,1)} %bitcast.10), kind=kLoop, calls=%fused_computation | loop fusion | bytes 102400 | tf_op jit(solution)/shard_map/broadcast_in_dim | solution.py:396
  101.1 2.7 %slice.8 = bf16[1536,512]{1,0:T(8,128)(2,1)} slice(bf16[1664,512]{1,0:T(8,128)(2,1)} %bitcast.11), slice={[0:1536], [0:512]} | slice | bytes 3145728 | tf_op jit(solution)/shard_map/slice | solution.py:395
  103.8 0.0 copy-done
  103.8 0.8 copy.11
Async XLA Ops:
  99.6 4.2 %copy-start = (bf16[4,128,512]{2,1,0:T(8,128)(2,1)S(1)}, bf16[4,128,512]{2,1,0:T(8,128)(2,1)}, u32[]{:S(2)}) copy-start(bf16[4,128,512]{2,1,0:T(8,128)(2,1)} %get-tuple-element.5) | copy-start | bytes 1572868
